TPU v7x, 32 devices: a whole 2x2x4 slice. The times are simulated.
32 devices in a mesh: cell: 16 (over z, x, core), gene: 2 (over y).
Axes of the slice: x: 2, y: 2, z: 4, core: 2. Of those that a mesh axis runs over, the one named last changes fastest.
Arguments:
- counts: bfloat16 [15360, 16384], P('cell', 'gene'), as said below
- w_factor: float32 [15360, 128], P('cell'), may hold values from 0.004 to 2, as said below
- h_factor: float32 [128, 16384], P('cell', 'gene'), may hold values from 0.03 to 0.3, as said below
Outputs:
- w_updated: float32 [15360, 128], P('cell')
- h_updated: float32 [128, 16384], P('cell', 'gene')
Inputs may be any that keep to these rules, and one draw needn't show every extreme that they name: `counts`: nonnegative whole numbers. `w_factor`: positive. `h_factor`: positive.
All inputs are finite; a program needn't handle non-finite values.
Results may differ from a plain program's by a relative error of at most 0.00092.
Values may be sent and summed in bfloat16 or wider, within the bound.
No kernel may reach another device: no remote copies, remote signals or barrier semaphores. Data moves between devices by JAX's collectives and lax.ppermute only.
A program may use at most 64 MiB of HBM per device.

v0:
```python
import jax
import jax.numpy as jnp
from jax import lax
from jax.sharding import PartitionSpec as P


def per_device(counts, w_factor, h_factor):
    own_rows = h_factor.shape[0]
    rank = w_factor.shape[1]
    w_copy = w_factor.astype(jnp.bfloat16)
    row_offset = lax.axis_index("cell") * own_rows
    counts_float = counts.astype(jnp.float32)
    columns = w_copy
    modeled = jnp.dot(
        columns,
        lax.all_gather(h_factor.astype(jnp.bfloat16), "cell", axis=0, tiled=True),
        preferred_element_type=jnp.float32,
    )
    quotient = (counts_float / modeled).astype(jnp.bfloat16)
    columns = w_copy
    numerator = lax.psum_scatter(
        lax.dot_general(
            columns, quotient, (((0,), (0,)), ((), ())), preferred_element_type=jnp.float32
        ),
        "cell",
        scatter_dimension=0,
        tiled=True,
    )
    w_totals = lax.psum(jnp.sum(w_factor, axis=0), "cell")
    own_totals = lax.dynamic_slice_in_dim(w_totals, row_offset, own_rows, 0)
    h_updated = h_factor * numerator / own_totals[:, None]
    h_new_copy = lax.all_gather(h_updated.astype(jnp.bfloat16), "cell", axis=0, tiled=True)
    modeled_again = jnp.dot(w_copy, h_new_copy, preferred_element_type=jnp.float32)
    quotient_again = (counts_float / modeled_again).astype(jnp.bfloat16)
    partial_w = lax.dot_general(
        quotient_again, h_new_copy, (((1,), (1,)), ((), ())), preferred_element_type=jnp.float32
    )
    partial_totals = jnp.sum(h_new_copy.astype(jnp.float32), axis=1)
    w_share = lax.psum_scatter(partial_w, "gene", scatter_dimension=1, tiled=True)
    h_totals = lax.psum(partial_totals, "gene")
    share_width = rank // lax.axis_size("gene")
    col_offset = lax.axis_index("gene") * share_width
    w_own = lax.dynamic_slice_in_dim(w_factor, col_offset, share_width, 1)
    totals_own = lax.dynamic_slice_in_dim(h_totals, col_offset, share_width, 0)
    w_part = w_own * w_share / totals_own[None, :]
    w_updated = lax.all_gather(w_part, "gene", axis=1, tiled=True)
    return (w_updated, h_updated)


def solution(mesh):
    in_specs = (P("cell", "gene"), P("cell", None), P("cell", "gene"))
    out_specs = (P("cell", None), P("cell", "gene"))
    return jax.shard_map(
        per_device, mesh=mesh, in_specs=in_specs, out_specs=out_specs, check_vma=False
    )
```

profile of v0, /device:TPU:0, one launch (start us, length us, event | category | flops | bytes accessed | tf_op | source)
XLA Modules:
  0.0 248.2 jit_solution(8995357598601707280)
XLA Ops:
  7.2 0.0 all-gather.3.cloned.1.call-start
  7.2 1.6 convert_element_type.23
  8.8 0.0 all-gather.3.cloned.1.call-update
  8.9 0.0 reduce-scatter.7.cloned.1.call-start
  8.9 46.0 %all-gather.3.cloned.1.call-done = bf16[128,8192]{1,0:T(8,128)(2,1)} async-done(((bf16[8,8192]{1,0:T(8,128)(2,1)}), bf16[128,8192]{1,0:T(8,128)(2,1)}) %all-gather.3.cloned.1.call-update) | async-done | bytes 2097168 | tf_op jit(solution)/shard_map/all_gather | solution.py:16
  54.9 16.7 %fusion.4 = f32[128,8192]{0,1:T(8,128)} fusion(bf16[960,8192]{1,0:T(8,128)(2,1)} %param.3, bf16[128,8192]{1,0:T(8,128)(2,1)} %all-gather.3.cloned.1.call-done, f32[960,128]{1,0:T(8,128)} %param.4), kind=kOutput, calls=%fused_computation.5 | convolution fusion | flops 4050370560 | bytes 22511616 | tf_op jit(solution)/shard_map/dot_general | solution.py:22
  71.6 5.6 %copy.14 = f32[128,8192]{1,0:T(8,128)} copy(f32[128,8192]{0,1:T(8,128)} %fusion.4) | data formatting | bytes 8388608
  77.2 0.0 copy-start.2
  77.3 0.0 copy-start.1
  77.3 0.0 reduce-scatter.7.cloned.1.call-update
  77.3 0.0 all-gather.5.cloned.1.call-start
  77.3 0.9 copy-done.2
  78.2 2.6 %copy.10 = f32[8,8192]{0,1:T(8,128)} copy(f32[8,8192]{1,0:T(8,128)S(1)} %copy-done.2) | data formatting | bytes 524288 | tf_op args[2]
  80.8 0.0 copy-done.1
  80.8 0.1 reduce_sum.18
  80.9 31.7 %psum.14 = f32[128]{0:T(128)S(1)} all-reduce(f32[128]{0:T(128)S(1)} %reduce_sum.18), channel_id=1, replica_groups=mesh['cell'=16,'gene'=2] {'cell'}, use_global_device_ids=true, to_apply=%region_2.0 | all-reduce | flops 128 | bytes 1024 | tf_op jit(solution)/shard_map/psum | solution.py:29
  112.6 0.1 dynamic_slice.10
  112.7 36.1 %reduce-scatter.7.cloned.1.call-done = f32[8,8192]{1,0:T(8,128)} async-done(((f32[128,8192]{1,0:T(8,128)}), f32[8,8192]{1,0:T(8,128)}) %reduce-scatter.7.cloned.1.call-update) | async-done | bytes 262160
  148.7 3.5 %copy.15 = f32[8,8192]{0,1:T(8,128)} copy(f32[8,8192]{1,0:T(8,128)} %reduce-scatter.7.cloned.1.call-done) | data formatting | bytes 524288
  152.2 5.9 %fusion.14 = (bf16[8,8192]{0,1:T(8,128)(2,1)S(1)}, f32[8,8192]{0,1:T(8,128)}) fusion(f32[8]{0:T(128)S(1)} %dynamic_slice.10, f32[8,8192]{0,1:T(8,128)} %copy.10, f32[8,8192]{0,1:T(8,128)} %copy.15), kind=kLoop, calls=%fused_computation.14 | loop fusion | flops 196608 | bytes 917536 | tf_op jit(solution)/shard_map/convert_element_type | solution.py:32
  158.1 1.4 copy.11
  159.5 0.0 all-gather.5.cloned.1.call-update
  159.6 0.2 reduce-scatter.5.cloned.1.call-start
  159.8 40.4 %all-gather.5.cloned.1.call-done = bf16[128,8192]{1,0:T(8,128)(2,1)} async-done(((bf16[8,8192]{1,0:T(8,128)(2,1)}), bf16[128,8192]{1,0:T(8,128)(2,1)}) %all-gather.5.cloned.1.call-update) | async-done | bytes 2097168 | tf_op jit(solution)/shard_map/all_gather | solution.py:32
  200.2 17.3 %fusion.9 = f32[960,128]{0,1:T(8,128)} fusion(bf16[128,8192]{1,0:T(8,128)(2,1)} %all-gather.5.cloned.1.call-done, bf16[960,8192]{1,0:T(8,128)(2,1)} %param.3, f32[960,128]{1,0:T(8,128)S(1)} %copy-done.1), kind=kOutput, calls=%fused_computation.7 | convolution fusion | flops 4050247680 | bytes 18808832 | tf_op jit(solution)/shard_map/dot_general | solution.py:35
  217.5 0.0 copy-start
  217.5 0.0 reduce-scatter.5.cloned.1.call-update
  217.5 0.2 constant_dynamic-slice_fusion
  217.7 0.2 copy.16
  217.9 3.7 %copy.13 = f32[8,8192]{1,0:T(8,128)} copy(f32[8,8192]{0,1:T(8,128)} %get-tuple-element.7) | data formatting | bytes 524288
  221.6 0.0 copy-done
  221.6 0.4 convert_reduce_fusion
  221.9 5.1 %psum.15 = f32[128]{0:T(128)S(1)} all-reduce(f32[128]{0:T(128)S(1)} %convert_reduce_fusion), channel_id=1, replica_groups=mesh['cell'=16,'gene'=2] {'gene'}, use_global_device_ids=true, to_apply=%region_5.0 | all-reduce | flops 128 | bytes 1024 | tf_op jit(solution)/shard_map/psum | solution.py:40
  227.1 0.1 dynamic_slice.11
  227.1 4.0 %reduce-scatter.5.cloned.1.call-done = f32[960,64]{0,1:T(8,128)} async-done(((f32[960,128]{0,1:T(8,128)}), f32[960,64]{0,1:T(8,128)}) %reduce-scatter.5.cloned.1.call-update) | async-done | bytes 245776 | tf_op jit(solution)/shard_map/reduce_scatter | solution.py:39
  231.1 1.0 multiply_divide_fusion.1
  232.1 8.5 %all_gather.11 = f32[960,128]{0,1:T(8,128)S(1)} all-gather(f32[960,64]{0,1:T(8,128)S(1)} %multiply_divide_fusion.1), channel_id=1, replica_groups=mesh['cell'=16,'gene'=2] {'gene'}, dimensions={1}, use_global_device_ids=true | all-gather | bytes 737280 | tf_op jit(solution)/shard_map/all_gather | solution.py:46
  240.7 1.0 copy.12
Async XLA Ops:
  7.2 47.8 %all-gather.3.cloned.1.call-start = ((), (), s32[]{:S(2)}) async-start(), calls=%async_computation.2 | async-start | bytes 2228224 | tf_op jit(solution)/shard_map/all_gather | solution.py:16
  8.9 139.9 %reduce-scatter.7.cloned.1.call-start = ((), (), s32[]{:S(2)}) async-start(), calls=%async_computation.5 | async-start | bytes 4456448
  77.2 0.9 copy-start.2
  77.3 3.5 %copy-start.1 = (f32[960,128]{1,0:T(8,128)S(1)}, f32[960,128]{1,0:T(8,128)}, u32[]{:S(2)}) copy-start(f32[960,128]{1,0:T(8,128)} %param.4) | copy-start | bytes 1474564
  77.3 122.9 %all-gather.5.cloned.1.call-start = ((), (), s32[]{:S(2)}) async-start(), calls=%async_computation.3 | async-start | bytes 2228224 | tf_op jit(solution)/shard_map/all_gather | solution.py:32
  159.6 71.5 %reduce-scatter.5.cloned.1.call-start = ((), (), s32[]{:S(2)}) async-start(), calls=%async_computation.4 | async-start | bytes 786432 | tf_op jit(solution)/shard_map/reduce_scatter | solution.py:39
  217.5 4.1 %copy-start = (bf16[128,8192]{1,0:T(8,128)(2,1)S(1)}, bf16[128,8192]{1,0:T(8,128)(2,1)}, u32[]{:S(2)}) copy-start(bf16[128,8192]{1,0:T(8,128)(2,1)} %all-gather.5.cloned.1.call-done) | copy-start | bytes 6291460
Sparse Core Ops, SparseCore 0:
  10.7 44.1 all-gather.2
  77.4 71.2 reduce-scatter.6
  159.7 40.4 all-gather.4
  217.6 13.4 reduce-scatter.4
where the time goes:
time: 249 us; the launch traced here: 248 us
  waiting for transfers between devices  126 us (51%)
  blocking collectives  45.4 us (18%)
  matrix products  34 us (14%)
  local copies, waits for them, and re-layouts  19.2 us (8%)
  between operations  13.8 us (6%)
  other arithmetic  9.09 us (4%)
    all_gather x1, waiting for transfers between devices, per_device(): lax.all_gather(h_factor.astype(jnp.bfloat16), 'cell', axis=0, tiled=True)  46 us
    all_gather x1, waiting for transfers between devices, per_device(): lax.all_gather(h_updated.astype(jnp.bfloat16), 'cell', axis=0, tiled=True)  40.4 us
    unnamed x5, waiting for transfers between devices  36.1 us
    psum x1, blocking collectives, per_device(): w_totals = lax.psum(jnp.sum(w_factor, axis=0), 'cell')  31.7 us
    unnamed x12, local copies, waits for them, and re-layouts  17.4 us
    dot_general x1, matrix products, per_device(): lax.dot_general(quotient_again, h_new_copy, (((1,), (1,)), ((), ())), pre...  17.3 us
    dot_general x1, matrix products, per_device(): lax.dot_general(columns, quotient, (((0,), (0,)), ((), ())), preferred_el...  16.7 us
    all_gather x1, blocking collectives, per_device(): w_updated = lax.all_gather(w_part, 'gene', axis=1, tiled=True)  8.55 us
  transfers between devices with their start and end apart: 4, of which 4 were waited for; matrix products, arithmetic and copies ran while one was open for 3% of the time, Pallas kernels for 0%

commit v1 on v0

--- a/solution.py
+++ b/solution.py
@@ -2,6 +2,23 @@
 import jax.numpy as jnp
 from jax import lax
 from jax.sharding import PartitionSpec as P
+
+
+def laid_out(parts, dim):
+    parts = jnp.moveaxis(parts, 0, dim)
+    dims = parts.shape
+    return parts.reshape(*dims[:dim], dims[dim] * dims[dim + 1], *dims[dim + 2 :])
+
+
+def collected_by_bits(value, axis):
+    devices, index = (lax.axis_size(axis), lax.axis_index(axis))
+    pieces, bit = (value[None], 1)
+    while bit < devices:
+        other = lax.ppermute(pieces, axis, [(i, i ^ bit) for i in range(devices)])
+        low = index & bit == 0
+        pieces = jnp.concatenate([jnp.where(low, pieces, other), jnp.where(low, other, pieces)])
+        bit *= 2
+    return pieces
 
 
 def per_device(counts, w_factor, h_factor):
@@ -29,7 +46,8 @@
     w_totals = lax.psum(jnp.sum(w_factor, axis=0), "cell")
     own_totals = lax.dynamic_slice_in_dim(w_totals, row_offset, own_rows, 0)
     h_updated = h_factor * numerator / own_totals[:, None]
-    h_new_copy = lax.all_gather(h_updated.astype(jnp.bfloat16), "cell", axis=0, tiled=True)
+    shard = h_updated.astype(jnp.bfloat16)
+    h_new_copy = laid_out(collected_by_bits(shard, "cell"), 0)
     modeled_again = jnp.dot(w_copy, h_new_copy, preferred_element_type=jnp.float32)
     quotient_again = (counts_float / modeled_again).astype(jnp.bfloat16)
     partial_w = lax.dot_general(

time: 249 us -> 284 us (1.14)
  waiting for transfers between devices: 126 us -> 153 us
  other arithmetic: 9.09 us -> 14.6 us
  local copies, waits for them, and re-layouts: 19.2 us -> 23.8 us
  matrix products: 34 us -> 29.9 us
    ppermute x0 -> x4, waiting for transfers between devices: none -> 67.2 us  [collected_by_bits(): other = lax.ppermute(pieces, axis, [(i, i ^ bit) for i in range(devices)])]
    all_gather x1 -> x0, waiting for transfers between devices: 40.4 us -> none  [per_device(): lax.all_gather(h_updated.astype(jnp.bfloat16), 'cell', axis=0, tiled=True)]
    broadcast_in_dim x0 -> x1, other arithmetic: none -> 5.95 us  [collected_by_bits(): pieces, bit = (value[None], 1)]
    convert_element_type x1 -> x0, other arithmetic: 5.94 us -> none  [per_device(): h_updated.astype(jnp.bfloat16)]
    select_n x0 -> x4, other arithmetic: none -> 5.31 us  [collected_by_bits(): jnp.where(low, pieces, other)]
    dot_general x1, matrix products: 17.3 us -> 13.2 us  [per_device(): lax.dot_general(quotient_again, h_new_copy, (((1,), (1,)), ((), ())), pre...]
    select_n x0 -> x2, local copies, waits for them, and re-layouts: none -> 3.69 us  [the longest x1 1.85 us: collected_by_bits(): jnp.where(low, other, pieces)]
    ppermute x0 -> x4, starting transfers between devices: none -> 2.88 us  [collected_by_bits(): other = lax.ppermute(pieces, axis, [(i, i ^ bit) for i in range(devices)])]
  transfers between devices with their start and end apart: 4 -> 7, of which waited for: 4 -> 7; matrix products, arithmetic and copies ran while one was open for 3% -> 3% of each run, Pallas kernels for 0% -> 0%
where the time goes in v1:
time: 284 us
  waiting for transfers between devices  153 us (54%)
  blocking collectives  45.7 us (16%)
  matrix products  29.9 us (11%)
  local copies, waits for them, and re-layouts  23.8 us (8%)
  other arithmetic  14.6 us (5%)
  between operations  13.8 us (5%)
  starting transfers between devices  3.01 us (1%)
    ppermute x4, waiting for transfers between devices, collected_by_bits(): other = lax.ppermute(pieces, axis, [(i, i ^ bit) for i in range(devices)])  67.2 us
    all_gather x1, waiting for transfers between devices, per_device(): lax.all_gather(h_factor.astype(jnp.bfloat16), 'cell', axis=0, tiled=True)  46 us
    unnamed x4, waiting for transfers between devices  35.8 us
    psum x1, blocking collectives, per_device(): w_totals = lax.psum(jnp.sum(w_factor, axis=0), 'cell')  32 us
    unnamed x12, local copies, waits for them, and re-layouts  17.2 us
    dot_general x1, matrix products, per_device(): lax.dot_general(columns, quotient, (((0,), (0,)), ((), ())), preferred_el...  16.7 us
    dot_general x1, matrix products, per_device(): lax.dot_general(quotient_again, h_new_copy, (((1,), (1,)), ((), ())), pre...  13.2 us
    all_gather x1, blocking collectives, per_device(): w_updated = lax.all_gather(w_part, 'gene', axis=1, tiled=True)  8.55 us
  transfers between devices with their start and end apart: 7, of which 7 were waited for; matrix products, arithmetic and copies ran while one was open for 3% of the time, Pallas kernels for 0%

profile of v1, /device:TPU:0, one launch (start us, length us, event | category | flops | bytes accessed | tf_op | source)
XLA Modules:
  0.0 283.9 jit_solution(13033812407531663100)
XLA Ops:
  7.2 0.0 all-gather.2.cloned.1.call-start
  7.2 1.6 convert_element_type.24
  8.8 0.0 all-gather.2.cloned.1.call-update
  8.9 0.0 reduce-scatter.7.cloned.1.call-start
  8.9 46.0 %all-gather.2.cloned.1.call-done = bf16[128,8192]{1,0:T(8,128)(2,1)} async-done(((bf16[8,8192]{1,0:T(8,128)(2,1)}), bf16[128,8192]{1,0:T(8,128)(2,1)}) %all-gather.2.cloned.1.call-update) | async-done | bytes 2097168 | tf_op jit(solution)/shard_map/all_gather | solution.py:33
  54.9 16.7 %fusion.4 = f32[128,8192]{0,1:T(8,128)} fusion(bf16[960,8192]{1,0:T(8,128)(2,1)} %param.3, bf16[128,8192]{1,0:T(8,128)(2,1)} %all-gather.2.cloned.1.call-done, f32[960,128]{1,0:T(8,128)} %param.4), kind=kOutput, calls=%fused_computation.5 | convolution fusion | flops 4050370560 | bytes 22511616 | tf_op jit(solution)/shard_map/dot_general | solution.py:39
  71.6 5.6 %copy.23 = f32[128,8192]{1,0:T(8,128)} copy(f32[128,8192]{0,1:T(8,128)} %fusion.4) | data formatting | bytes 8388608
  77.2 0.0 reduce-scatter.7.cloned.1.call-update
  77.2 0.0 reduce-scatter.5.cloned.1.call-start
  77.3 0.9 copy-done.2
  78.1 2.6 copy.15
  80.7 0.0 copy-done
  80.7 0.1 reduce_sum.20
  80.9 32.0 %psum.14 = f32[128]{0:T(128)S(1)} all-reduce(f32[128]{0:T(128)S(1)} %reduce_sum.20), channel_id=1, replica_groups=mesh['cell'=16,'gene'=2] {'cell'}, use_global_device_ids=true, to_apply=%region_2.0 | all-reduce | flops 128 | bytes 1024 | tf_op jit(solution)/shard_map/psum | solution.py:46
  112.8 0.1 dynamic_slice.10
  112.9 35.8 %reduce-scatter.7.cloned.1.call-done = f32[8,8192]{1,0:T(8,128)} async-done(((f32[128,8192]{1,0:T(8,128)}), f32[8,8192]{1,0:T(8,128)}) %reduce-scatter.7.cloned.1.call-update) | async-done | bytes 262160
  148.7 3.5 %copy.24 = f32[8,8192]{0,1:T(8,128)} copy(f32[8,8192]{1,0:T(8,128)} %reduce-scatter.7.cloned.1.call-done) | data formatting | bytes 524288
  152.2 6.0 %convert_bitcast_fusion = (bf16[1,8,8192]{1,2,0:T(8,128)(2,1)S(1)}, f32[8,8192]{0,1:T(8,128)}) fusion(f32[8]{0:T(128)S(1)} %dynamic_slice.10, f32[8,8192]{0,1:T(8,128)} %copy.15, f32[8,8192]{0,1:T(8,128)} %copy.24), kind=kLoop, calls=%fused_computation.12 | loop fusion | flops 196608 | bytes 917536 | tf_op jit(solution)/shard_map/broadcast_in_dim | solution.py:15
  158.1 0.8 copy.16
  158.9 0.1 collective-permute-start
  159.0 1.3 collective-permute-done
  160.3 1.7 copy.17
  162.0 3.8 %broadcast_select_fusion.1 = (bf16[1,8,8192]{1,2,0:T(8,128)(2,1)}, bf16[1,8,8192]{1,2,0:T(8,128)(2,1)}) fusion(bf16[1,8,8192]{1,2,0:T(8,128)(2,1)S(1)} %get-tuple-element.8, bf16[1,8,8192]{1,2,0:T(8,128)(2,1)} %copy.17, pred[]{:T(512)S(6)} %eq.15), kind=kLoop, calls=%fused_computation.14 | loop fusion | flops 131072 | bytes 524289 | tf_op jit(solution)/shard_map/jit(_where)/select_n | solution.py:19
  165.8 1.8 copy.19
  167.7 1.9 copy.20
  169.6 0.5 collective-permute-start.1
  170.1 7.9 %collective-permute-done.1 = bf16[2,8,8192]{2,1,0:T(8,128)(2,1)S(1)} collective-permute-done((bf16[2,8,8192]{2,1,0:T(8,128)(2,1)S(1)}, bf16[2,8,8192]{2,1,0:T(8,128)(2,1)S(1)}, u32[]{:S(2)}, u32[]{:S(2)}) %collective-permute-start.1) | collective-permute-done | bytes 262176 | tf_op jit(solution)/shard_map/ppermute | solution.py:17
  178.1 1.0 collective-permute-start.2
  179.1 12.2 %collective-permute-done.2 = bf16[4,8,8192]{2,1,0:T(8,128)(2,1)S(1)} collective-permute-done((bf16[4,8,8192]{2,1,0:T(8,128)(2,1)S(1)}, bf16[4,8,8192]{2,1,0:T(8,128)(2,1)S(1)}, u32[]{:S(2)}, u32[]{:S(2)}) %collective-permute-start.2) | collective-permute-done | bytes 524320 | tf_op jit(solution)/shard_map/ppermute | solution.py:17
  191.3 0.1 broadcast_select_fusion.5
  191.4 0.1 pad_maximum_fusion.3
  191.5 1.3 collective-permute-start.3
  192.8 45.7 %collective-permute-done.3 = bf16[8,8,8192]{2,1,0:T(8,128)(2,1)} collective-permute-done((bf16[8,8,8192]{2,1,0:T(8,128)(2,1)S(1)}, bf16[8,8,8192]{2,1,0:T(8,128)(2,1)}, u32[]{:S(2)}, u32[]{:S(2)}) %collective-permute-start.3) | collective-permute-done | bytes 1048608 | tf_op jit(solution)/shard_map/ppermute | solution.py:17
  238.5 1.4 broadcast_select_fusion.3
  239.9 0.0 copy-start.1
  239.9 13.2 %fusion.9 = f32[960,128]{0,1:T(8,128)} fusion(bf16[960,8192]{1,0:T(8,128)(2,1)} %param.3, bf16[8,8,8192]{2,1,0:T(8,128)(2,1)S(1)} %get-tuple-element.13, bf16[8,8,8192]{2,1,0:T(8,128)(2,1)S(1)} %get-tuple-element.12, f32[960,128]{1,0:T(8,128)} %param.4), kind=kOutput, calls=%fused_computation.7 | convolution fusion | flops 4052344832 | bytes 18808832 | tf_op jit(solution)/shard_map/dot_general | solution.py:53
  253.1 0.0 reduce-scatter.5.cloned.1.call-update
  253.2 0.2 constant_dynamic-slice_fusion
  253.4 0.2 copy.25
  253.5 3.5 %copy.22 = f32[8,8192]{1,0:T(8,128)} copy(f32[8,8192]{0,1:T(8,128)} %get-tuple-element.9) | data formatting | bytes 524288
  257.0 0.4 convert_reduce_fusion
  257.4 0.1 reduce_sum.22
  257.5 5.1 %psum.15 = f32[128]{0:T(128)S(1)} all-reduce(f32[128]{0:T(128)S(1)} %reduce_sum.22), channel_id=1, replica_groups=mesh['cell'=16,'gene'=2] {'gene'}, use_global_device_ids=true, to_apply=%region_5.6 | all-reduce | flops 128 | bytes 1024 | tf_op jit(solution)/shard_map/psum | solution.py:58
  262.6 0.1 dynamic_slice.11
  262.7 4.1 %reduce-scatter.5.cloned.1.call-done = f32[960,64]{0,1:T(8,128)} async-done(((f32[960,128]{0,1:T(8,128)}), f32[960,64]{0,1:T(8,128)}) %reduce-scatter.5.cloned.1.call-update) | async-done | bytes 245776 | tf_op jit(solution)/shard_map/reduce_scatter | solution.py:57
  266.8 1.0 multiply_divide_fusion.1
  267.9 8.6 %all_gather.7 = f32[960,128]{0,1:T(8,128)S(1)} all-gather(f32[960,64]{0,1:T(8,128)S(1)} %multiply_divide_fusion.1), channel_id=1, replica_groups=mesh['cell'=16,'gene'=2] {'gene'}, dimensions={1}, use_global_device_ids=true | all-gather | bytes 737280 | tf_op jit(solution)/shard_map/all_gather | solution.py:64
  276.4 1.0 copy.21
  (6 shorter events, 0.1 us)
Async XLA Ops:
  7.2 47.8 %all-gather.2.cloned.1.call-start = ((), (), s32[]{:S(2)}) async-start(), calls=%async_computation.2 | async-start | bytes 2228224 | tf_op jit(solution)/shard_map/all_gather | solution.py:33
  8.9 139.8 %reduce-scatter.7.cloned.1.call-start = ((), (), s32[]{:S(2)}) async-start(), calls=%async_computation.4 | async-start | bytes 4456448
  77.2 0.9 copy-start.2
  77.2 3.5 %copy-start = (f32[960,128]{1,0:T(8,128)S(1)}, f32[960,128]{1,0:T(8,128)}, u32[]{:S(2)}) copy-start(f32[960,128]{1,0:T(8,128)} %param.4) | copy-start | bytes 1474564
  77.2 189.6 %reduce-scatter.5.cloned.1.call-start = ((), (), s32[]{:S(2)}) async-start(), calls=%async_computation.3 | async-start | bytes 786432 | tf_op jit(solution)/shard_map/reduce_scatter | solution.py:57
  158.9 1.4 collective-permute-start
  169.6 8.4 %collective-permute-start.1 = (bf16[2,8,8192]{2,1,0:T(8,128)(2,1)S(1)}, bf16[2,8,8192]{2,1,0:T(8,128)(2,1)S(1)}, u32[]{:S(2)}, u32[]{:S(2)}) collective-permute-start(bf16[2,8,8192]{2,1,0:T(8,128)(2,1)S(1)} %pad_maximum_fusion.5), channel_id=1, source_target_pairs={{0,4},{2,6},{4,0},{6,2},{8,12},{10,14},{12,8},{14,10},{16,20},{18,... | collective-permute-start | bytes 786440 | tf_op jit(solution)/shard_map/ppermute | solution.py:17
  178.1 13.2 %collective-permute-start.2 = (bf16[4,8,8192]{2,1,0:T(8,128)(2,1)S(1)}, bf16[4,8,8192]{2,1,0:T(8,128)(2,1)S(1)}, u32[]{:S(2)}, u32[]{:S(2)}) collective-permute-start(bf16[4,8,8192]{2,1,0:T(8,128)(2,1)S(1)} %pad_maximum_fusion.4), channel_id=1, source_target_pairs={{0,8},{2,10},{4,12},{6,14},{8,0},{10,2},{12,4},{14,6},{16,24},{18,... | collective-permute-start | bytes 1572872 | tf_op jit(solution)/shard_map/ppermute | solution.py:17
  191.5 47.0 %collective-permute-start.3 = (bf16[8,8,8192]{2,1,0:T(8,128)(2,1)S(1)}, bf16[8,8,8192]{2,1,0:T(8,128)(2,1)}, u32[]{:S(2)}, u32[]{:S(2)}) collective-permute-start(bf16[8,8,8192]{2,1,0:T(8,128)(2,1)S(1)} %pad_maximum_fusion.3), channel_id=1, source_target_pairs={{0,16},{2,18},{4,20},{6,22},{8,24},{10,26},{12,28},{14,30},{16,0},... | collective-permute-start | bytes 3145736 | tf_op jit(solution)/shard_map/ppermute | solution.py:17
  239.9 13.3 %copy-start.1 = (f32[960,128]{1,0:T(8,128)S(1)}, f32[960,128]{1,0:T(8,128)}, u32[]{:S(2)}) copy-start(f32[960,128]{1,0:T(8,128)} %param.4) | copy-start | bytes 1474564
Sparse Core Ops, SparseCore 0:
  10.7 44.1 all-gather.1
  77.3 71.2 reduce-scatter.6
  253.3 13.5 reduce-scatter.4
